TPU v7x, 32 devices: a whole 2x2x4 slice. The times are simulated.
32 devices in a mesh: dp: 16 (over z, x, core), head: 2 (over y).
Axes of the slice: x: 2, y: 2, z: 4, core: 2. Of those that a mesh axis runs over, the one named last changes fastest.
Arguments:
- x_input: bfloat16 [2048, 8192], P('dp'), may hold values from -8 to 8
- wq_old: bfloat16 [8192, 1024], P('dp', 'head'), may hold values from -0.0625 to 0.0625
- wq_fresh: bfloat16 [8192, 256], P('dp', 'head'), may hold values from -0.0625 to 0.0625
- key_projection_weight: bfloat16 [8192, 256], P('dp', 'head'), may hold values from -0.0625 to 0.0625
- value_projection_weight: bfloat16 [8192, 256], P('dp', 'head'), may hold values from -0.0625 to 0.0625
- attention_output_gradient: bfloat16 [2048, 1280], P('dp', 'head'), may hold values from -6 to 6
- head_source: int32 [10], replicated, may hold values from 0 to 9, as said below
- doc_ids: int32 [2048], P('dp'), may hold values from 0 to 63, never falling along the last dimension, each value on 1 to 128 neighbouring positions
Outputs:
- attn_out: bfloat16 [2048, 1280], P('dp', 'head')
- x_grad: bfloat16 [2048, 8192], P('dp', 'head')
Inputs may be any that keep to these rules, and one draw needn't show every extreme that they name: head_source is a permutation. There are shifts s_k and a permutation t of the 5 local indices, the same for every owner d, such that new head d * 5 + k takes candidate ((d - s_k) mod 2) * 5 + t_k; one owner takes at most 3 new head from any one former owner, and some pair reaches 3.
All inputs are finite; a program needn't handle non-finite values.
Results may differ from a plain program's by a relative error of at most 0.014.
The roundings to bfloat16 on the way count: a program that leaves them out, or rounds other values in their place, can miss the bound.
Values may be sent and summed in bfloat16 or wider, within the bound.
A program may use at most 64 MiB of HBM per device.

v0:
```python
import math

import jax
import jax.numpy as jnp
from jax import lax
from jax.sharding import PartitionSpec as P

theta_base = 500000.0
neg_large = -1e30


def rotary_tables(length, head_width):
    half_dim = head_width // 2
    frequency = theta_base ** (-2.0 * jnp.arange(half_dim, dtype=jnp.float32) / head_width)
    angles = jnp.arange(length, dtype=jnp.float32)[:, None] * frequency[None, :]
    return (jnp.cos(angles), jnp.sin(angles))


def rotate(field, cosine, sine_table):
    half_dim = field.shape[-1] // 2
    lower_half = field[..., :half_dim]
    upper_half = field[..., half_dim:]
    cosine = cosine[:, None, :]
    sine_table = sine_table[:, None, :]
    return jnp.concatenate(
        [
            lower_half * cosine - upper_half * sine_table,
            upper_half * cosine + lower_half * sine_table,
        ],
        axis=-1,
    )


def rotate_back(field, cosine, sine_table):
    half_dim = field.shape[-1] // 2
    lower_half = field[..., :half_dim]
    upper_half = field[..., half_dim:]
    cosine = cosine[:, None, :]
    sine_table = sine_table[:, None, :]
    return jnp.concatenate(
        [
            lower_half * cosine + upper_half * sine_table,
            upper_half * cosine - lower_half * sine_table,
        ],
        axis=-1,
    )


def routing(head_source, group_size, head_count, head_place):
    row_zero = head_source[:group_size]
    taken_index = row_zero % group_size
    shifts = (head_count - row_zero // group_size) % head_count
    local_ids = jnp.arange(group_size)
    earlier = local_ids[:, None] > local_ids[None, :]
    same_shift = shifts[:, None] == shifts[None, :]
    slot_index = jnp.sum((earlier & same_shift).astype(jnp.int32), axis=1)
    capacity = (group_size + head_count - 1) // head_count
    target = (head_place + shifts) % head_count
    anchor = (head_place - shifts + head_count) % head_count
    owners = jnp.arange(head_count)
    slots = jnp.arange(capacity)
    send_table = (
        (target[:, None, None, None] == owners[None, :, None, None])
        & (slot_index[:, None, None, None] == slots[None, None, :, None])
        & (taken_index[:, None, None, None] == local_ids[None, None, None, :])
    )
    sending = jnp.sum(send_table.astype(jnp.float32), axis=0).astype(jnp.bfloat16)
    receiving = (
        (anchor[:, None, None] == owners[None, :, None])
        & (slot_index[:, None, None] == slots[None, None, :])
    ).astype(jnp.bfloat16)
    return (sending, receiving)


def attention_pair(queries, key_rot, values, cotangent, doc_rows):
    length = queries.shape[0]
    scale_factor = 1.0 / math.sqrt(queries.shape[-1])
    scores = (
        jnp.einsum("qhd,kd->hqk", queries, key_rot, preferred_element_type=jnp.float32)
        * scale_factor
    )
    positions = jnp.arange(length)
    allowed = (positions[None, :] <= positions[:, None]) & (doc_rows[None, :] == doc_rows[:, None])
    scores = jnp.where(allowed[None], scores, neg_large)
    row_maximum = jnp.max(scores, axis=-1, keepdims=True)
    weights = jnp.exp(scores - row_maximum)
    probability = weights / jnp.sum(weights, axis=-1, keepdims=True)
    prob_b = probability.astype(jnp.bfloat16)
    output = jnp.einsum("hqk,kd->qhd", prob_b, values, preferred_element_type=jnp.float32).astype(
        jnp.bfloat16
    )
    prob_grad = jnp.einsum("qhd,kd->hqk", cotangent, values, preferred_element_type=jnp.float32)
    centre = jnp.sum(probability * prob_grad, axis=-1, keepdims=True)
    dscore = (probability * (prob_grad - centre) * scale_factor).astype(jnp.bfloat16)
    dquery = jnp.einsum("hqk,kd->qhd", dscore, key_rot, preferred_element_type=jnp.float32)
    key_grad = jnp.einsum("hqk,qhd->kd", dscore, queries, preferred_element_type=jnp.float32)
    dvalue = jnp.einsum("hqk,qhd->kd", prob_b, cotangent, preferred_element_type=jnp.float32)
    return (output, dquery, key_grad, dvalue)


def local(
    x_input,
    wq_old,
    wq_fresh,
    key_projection_weight,
    value_projection_weight,
    attention_output_gradient,
    head_source,
    doc_ids,
):
    length = x_input.shape[0]
    shard_rows = wq_old.shape[0]
    head_dim = key_projection_weight.shape[1]
    group_size = attention_output_gradient.shape[1] // head_dim
    head_count = lax.axis_size("head")
    head_place = lax.axis_index("head")
    sending, receiving = routing(head_source, group_size, head_count, head_place)
    own_heads = jnp.concatenate(
        [wq_old.reshape(shard_rows, -1, head_dim), wq_fresh.reshape(shard_rows, -1, head_dim)],
        axis=1,
    )
    parcel = jnp.einsum(
        "ecm,rmd->ecrd", sending, own_heads, preferred_element_type=jnp.float32
    ).astype(jnp.bfloat16)
    arrived = lax.all_to_all(parcel, "head", split_axis=0, concat_axis=0, tiled=True)
    local_heads = jnp.einsum(
        "kec,ecrd->rkd", receiving, arrived, preferred_element_type=jnp.float32
    ).astype(jnp.bfloat16)
    wq_full, wk_full, wv_full = (
        lax.all_gather(
            local_heads.reshape(shard_rows, group_size * head_dim), "dp", axis=0, tiled=True
        ),
        lax.all_gather(key_projection_weight, "dp", axis=0, tiled=True),
        lax.all_gather(value_projection_weight, "dp", axis=0, tiled=True),
    )
    cosine, sine_table = rotary_tables(length, head_dim)
    projected = jnp.dot(x_input, wq_full, preferred_element_type=jnp.float32).reshape(
        length, group_size, head_dim
    )
    queries = rotate(projected, cosine, sine_table).astype(jnp.bfloat16)
    key_proj = jnp.dot(x_input, wk_full, preferred_element_type=jnp.float32)
    key_rot = rotate(key_proj[:, None, :], cosine, sine_table)[:, 0, :].astype(jnp.bfloat16)
    values = jnp.dot(x_input, wv_full, preferred_element_type=jnp.float32).astype(jnp.bfloat16)
    cotangent = attention_output_gradient.reshape(length, group_size, head_dim)
    output, dquery, key_grad, dvalue = attention_pair(queries, key_rot, values, cotangent, doc_ids)
    dquery = rotate_back(dquery, cosine, sine_table).astype(jnp.bfloat16)
    key_grad = rotate_back(key_grad[:, None, :], cosine, sine_table)[:, 0, :].astype(jnp.bfloat16)
    dvalue = dvalue.astype(jnp.bfloat16)
    partial_grad = jnp.einsum(
        "sc,wc->sw",
        dquery.reshape(length, group_size * head_dim),
        wq_full,
        preferred_element_type=jnp.float32,
    )
    partial_grad = partial_grad + jnp.einsum(
        "sc,wc->sw", key_grad, wk_full, preferred_element_type=jnp.float32
    )
    partial_grad = partial_grad + jnp.einsum(
        "sc,wc->sw", dvalue, wv_full, preferred_element_type=jnp.float32
    )
    x_grad = lax.psum_scatter(
        partial_grad.astype(jnp.bfloat16), "head", scatter_dimension=1, tiled=True
    )
    return (output.reshape(length, group_size * head_dim), x_grad)


def solution(mesh):
    in_specs = (
        P("dp", None),
        P("dp", "head"),
        P("dp", "head"),
        P("dp", "head"),
        P("dp", "head"),
        P("dp", "head"),
        P(),
        P("dp"),
    )
    out_specs = (P("dp", "head"), P("dp", "head"))
    return jax.shard_map(local, mesh=mesh, in_specs=in_specs, out_specs=out_specs, check_vma=False)
```

profile of v0, /device:TPU:0, one launch (start us, length us, event | category | flops | bytes accessed | tf_op | source)
XLA Modules:
  0.0 252.3 jit_solution(8434962283655257791)
XLA Ops:
  7.2 0.7 all-gather.6.cloned.1.call-update
  8.0 0.7 all-gather.4.cloned.1.call-update
  8.7 0.7 and_select_fusion
  9.7 1.1 copy.77
  10.8 1.2 reshape.261
  12.2 1.0 convolution_convert_fusion
  13.2 1.0 copy.79
  14.2 4.3 %all-to-all-start = ((bf16[2,3,512,128]{3,2,1,0:T(8,128)(2,1)}), bf16[2,3,512,128]{3,2,1,0:T(8,128)(2,1)}, u32[]{:S(2)}, u32[]{:S(2)}) async-start(bf16[2,3,512,128]{3,2,1,0:T(8,128)(2,1)} %copy.79), calls=%async_computation | async-start | bytes 1572864 | tf_op jit(solution)/shard_map/all_to_all | solution.py:125
  18.6 12.3 %all-to-all-done = bf16[2,3,512,128]{3,2,1,0:T(8,128)(2,1)} async-done(((bf16[2,3,512,128]{3,2,1,0:T(8,128)(2,1)}), bf16[2,3,512,128]{3,2,1,0:T(8,128)(2,1)}, u32[]{:S(2)}, u32[]{:S(2)}) %all-to-all-start) | async-done | bytes 786464 | tf_op jit(solution)/shard_map/all_to_all | solution.py:125
  30.9 2.1 fusion.3
  32.9 1.3 copy.81
  35.1 19.4 %all-gather.6.cloned.1.call-done = bf16[8192,128]{1,0:T(8,128)(2,1)} async-done(((bf16[512,128]{1,0:T(8,128)(2,1)}), bf16[8192,128]{1,0:T(8,128)(2,1)}) %all-gather.6.cloned.1.call-update) | async-done | bytes 2097168 | tf_op jit(solution)/shard_map/all_gather | solution.py:133
  54.4 2.5 convolution_bitcast_fusion.4
  57.0 0.8 subtract_convert_fusion.3
  57.8 39.0 %all-gather.4.cloned.1.call-done = bf16[8192,128]{1,0:T(8,128)(2,1)} async-done(((bf16[512,128]{1,0:T(8,128)(2,1)}), bf16[8192,128]{1,0:T(8,128)(2,1)}) %all-gather.4.cloned.1.call-update) | async-done | bytes 2097168 | tf_op jit(solution)/shard_map/all_gather | solution.py:134
  96.8 2.3 fusion.13
  99.3 0.4 copy-done.4
  99.7 88.9 %all-gather.8.cloned.1.call-done = bf16[8192,640]{0,1:T(8,128)(2,1)} async-done(((bf16[512,640]{0,1:T(8,128)(2,1)}), bf16[8192,640]{0,1:T(8,128)(2,1)}) %all-gather.8.cloned.1.call-update) | async-done | bytes 10485776 | tf_op jit(solution)/shard_map/all_gather | solution.py:130
  188.6 5.6 %fusion.60 = f32[640,128]{1,0:T(8,128)S(1)} fusion(bf16[8192,640]{0,1:T(8,128)(2,1)} %all-gather.8.cloned.1.call-done, bf16[128,8192]{1,0:T(8,128)(2,1)S(1)} %copy-done), kind=kOutput, calls=%fused_computation.106 | convolution fusion | flops 1342177280 | bytes 12910592 | tf_op jit(solution)/shard_map/dot_general | solution.py:137
  194.6 0.8 subtract_convert_fusion.1
  195.3 1.3 fusion.59
  196.7 0.6 copy-done.9
  197.3 1.9 convolution_bitcast_fusion.3
  199.2 1.1 convolution_bitcast_fusion
  200.2 1.0 add_convert_fusion.2
  201.7 6.0 %fusion.61 = f32[128,8192]{1,0:T(8,128)S(1)} fusion(bf16[128,640]{0,1:T(8,128)(2,1)S(1)} %bitcast.97, bf16[8192,640]{0,1:T(8,128)(2,1)} %all-gather.8.cloned.1.call-done), kind=kOutput, calls=%fused_computation.107 | convolution fusion | flops 1342177280 | bytes 14843904 | tf_op jit(solution)/shard_map/sc,wc->sw/dot_general | solution.py:149
  207.7 2.7 %convolution_add_fusion.1 = f32[128,8192]{1,0:T(8,128)} fusion(f32[128,8192]{1,0:T(8,128)S(1)} %fusion.61, bf16[8192,128]{1,0:T(8,128)(2,1)S(1)} %copy-done.1, bf16[128,1,64]{0,2,1:T(8,128)(2,1)S(1)} %get-tuple-element.21, bf16[128,1,64]{0,2,1:T(8,128)(2,1)S(1)} %get-tuple-element.20), kind=kOutput, calls=%fused_computation.3 | convolution fusion | flops 269549568 | bytes 10518528 | tf_op jit(solution)/shard_map/sc,wc->sw/dot_general | solution.py:155
  210.4 5.0 %fusion.2 = bf16[128,8192]{1,0:T(8,128)(2,1)} fusion(f32[128,8192]{1,0:T(8,128)} %convolution_add_fusion.1, bf16[8192,128]{1,0:T(8,128)(2,1)} %all-gather.4.cloned.1.call-done, bf16[128,5,128]{0,2,1:T(8,128)(2,1)S(1)} %bitcast.96, f32[5,128,128]{1,2,0:T(8,128)S(1)} %get-tuple-element.28, f32[5,128]{1,0:T(8,128)S(1)} %copy-done.10), kind=kOutput, calls=%fused_computation.4 | convolution fusion | flops 291684352 | bytes 8882688 | tf_op jit(solution)/shard_map/sc,wc->sw/dot_general | solution.py:158
  215.5 0.9 copy-done.2
  216.4 0.5 convolution_convert_fusion.1
  216.9 0.8 copy.95
  217.7 28.0 %reduce-scatter.2.cloned.1.call-done = bf16[128,4096]{1,0:T(8,128)(2,1)} async-done(((bf16[128,8192]{1,0:T(8,128)(2,1)}), bf16[128,4096]{1,0:T(8,128)(2,1)}) %reduce-scatter.2.cloned.1.call-update) | async-done | bytes 1048592 | tf_op jit(solution)/shard_map/reduce_scatter | solution.py:161
  (47 shorter events, 2.5 us)
Async XLA Ops:
  7.2 47.3 %copy-start = (bf16[128,8192]{1,0:T(8,128)(2,1)S(1)}, bf16[128,8192]{1,0:T(8,128)(2,1)}, u32[]{:S(2)}) copy-start(bf16[128,8192]{1,0:T(8,128)(2,1)} %param.8) | copy-start | bytes 6291460
  7.2 47.3 %all-gather.6.cloned.1.call-start = ((), (), s32[]{:S(2)}) async-start(), calls=%async_computation.3 | async-start | bytes 2228224 | tf_op jit(solution)/shard_map/all_gather | solution.py:133
  7.9 88.9 %all-gather.4.cloned.1.call-start = ((), (), s32[]{:S(2)}) async-start(), calls=%async_computation.2 | async-start | bytes 2228224 | tf_op jit(solution)/shard_map/all_gather | solution.py:134
  14.2 16.7 %all-to-all-start = ((bf16[2,3,512,128]{3,2,1,0:T(8,128)(2,1)}), bf16[2,3,512,128]{3,2,1,0:T(8,128)(2,1)}, u32[]{:S(2)}, u32[]{:S(2)}) async-start(bf16[2,3,512,128]{3,2,1,0:T(8,128)(2,1)} %copy.79), calls=%async_computation | async-start | bytes 1572864 | tf_op jit(solution)/shard_map/all_to_all | solution.py:125
  18.5 170.1 %all-gather.8.cloned.1.call-start = ((), (), s32[]{:S(2)}) async-start(), calls=%async_computation.4 | async-start | bytes 11141120 | tf_op jit(solution)/shard_map/all_gather | solution.py:130
  18.5 16.0 %copy-start.3 = (bf16[128,640]{1,0:T(8,128)(2,1)S(1)}, bf16[128,640]{1,0:T(8,128)(2,1)}, u32[]{:S(2)}) copy-start(bf16[128,640]{1,0:T(8,128)(2,1)} %param.13) | copy-start | bytes 491524
  18.6 16.1 %copy-start.11 = (s32[128]{0:T(128)S(1)}, s32[128]{0:T(128)}, u32[]{:S(2)}) copy-start(s32[128]{0:T(128)} %param.15) | copy-start | bytes 1540
  34.3 211.5 %reduce-scatter.2.cloned.1.call-start = ((), (), s32[]{:S(2)}) async-start(), calls=%async_computation.5 | async-start | bytes 3145728 | tf_op jit(solution)/shard_map/reduce_scatter | solution.py:161
  34.7 22.3 %copy-start.8 = (f32[64]{0:T(128)}, f32[64]{0:T(128)S(1)}, u32[]{:S(2)}) copy-start(f32[64]{0:T(128)S(1)} %multiply_power_fusion) | copy-start | bytes 772
  99.1 0.6 copy-start.4
  196.7 0.6 copy-start.9
  201.7 6.0 %copy-start.1 = (bf16[8192,128]{1,0:T(8,128)(2,1)S(1)}, bf16[8192,128]{1,0:T(8,128)(2,1)}, u32[]{:S(2)}) copy-start(bf16[8192,128]{1,0:T(8,128)(2,1)} %all-gather.6.cloned.1.call-done) | copy-start | bytes 6291460
  207.7 2.7 %copy-start.10 = (f32[5,128]{1,0:T(8,128)S(1)}, f32[5,128]{1,0:T(8,128)}, u32[]{:S(2)}) copy-start(f32[5,128]{1,0:T(8,128)} %copy-done.9) | copy-start | bytes 7684
  215.5 0.9 copy-start.2
  215.5 0.9 copy-start.5
  215.5 0.9 copy-start.6
  215.5 0.9 copy-start.7
Sparse Core Ops, SparseCore 0:
  10.1 44.2 all-gather.5
  56.6 40.1 all-gather.3
  99.5 89.0 all-gather.7
  215.6 30.0 reduce-scatter.1
where the time goes:
time: 253 us; the launch traced here: 252 us
  waiting for transfers between devices  189 us (75%)
  matrix products  32.1 us (13%)
  between operations  14 us (6%)
  local copies, waits for them, and re-layouts  8.13 us (3%)
  starting transfers between devices  4.65 us (2%)
  other arithmetic  4.3 us (2%)
    all_gather x1, waiting for transfers between devices, local(): lax.all_gather(local_heads.reshape(shard_rows, group_size * head_dim), 'd...  88.9 us
    all_gather x1, waiting for transfers between devices, local(): lax.all_gather(value_projection_weight, 'dp', axis=0, tiled=True)  39 us
    reduce_scatter x1, waiting for transfers between devices, local(): lax.psum_scatter(partial_grad.astype(jnp.bfloat16), 'head', scatter_dimen...  28 us
    all_gather x1, waiting for transfers between devices, local(): lax.all_gather(key_projection_weight, 'dp', axis=0, tiled=True)  19.4 us
    all_to_all x1, waiting for transfers between devices, local(): lax.all_to_all(parcel, 'head', split_axis=0, concat_axis=0, tiled=True)  12.3 us
    dot_general x1, matrix products, local(): jnp.einsum('sc,wc->sw', dquery.reshape(length, group_size * head_dim), wq...  5.98 us
    dot_general x1, matrix products, local(): jnp.dot(x_input, wq_full, preferred_element_type=jnp.float32)  5.59 us
  transfers between devices with their start and end apart: 5, of which 5 were waited for; matrix products, arithmetic and copies ran while one was open for 7% of the time, Pallas kernels for 0%

commit v1 on v0

v1 whole, which is shorter than its diff:
```python
import functools
import math

import jax
import jax.numpy as jnp
import numpy as np
from jax import lax
from jax.experimental import pallas as pl
from jax.experimental.pallas import tpu as pltpu
from jax.sharding import PartitionSpec as P

theta_base = 500000.0
neg_large = -1e30
MESH = pl.DeviceIdType.MESH


def rotary_tables(length, width):
    half = width // 2
    frequency = theta_base ** (-2.0 * np.arange(half, dtype=np.float64) / width)
    angles = np.arange(length, dtype=np.float64)[:, None] * frequency[None, :]
    cosine, sine = np.cos(angles), np.sin(angles)
    return (
        np.concatenate([cosine, cosine], axis=1).astype(np.float32),
        np.concatenate([-sine, sine], axis=1).astype(np.float32),
    )


def dot(a, b, ca, cb):
    return lax.dot_general(
        a, b, (((ca,), (cb,)), ((), ())), preferred_element_type=jnp.float32
    )


def kernel(
    n_dp, n_head, group, ways,
    src_ref, doc_ref, cos_ref, sin_ref, x_hbm, old_hbm, fresh_hbm, k_hbm, v_hbm, g_hbm,
    out_ref, grad_ref,
    x_ref, own_ref, g_ref, wq, wkv, parcel, arrived, accq, acckv, dq_ref, dkv_ref,
    psend, precv,
    in_sem, rs, rr, cs, cr, hs, hr, ps, pr,
):
    me, head = lax.axis_index("dp"), lax.axis_index("head")
    rows, hd = k_hbm.shape
    length = x_ref.shape[0]
    lanes = 2
    m = n_dp // lanes
    core, chip = me % lanes, me // lanes
    side, level = chip % 2, chip // 2
    pos = (1 - side) * level + side * (m - 1 - level)
    piece = rows // ways
    capacity = parcel.shape[1]
    signs = (1, -1)[:ways]
    bufs = (wkv, wq)

    def index_of(p, lane):
        p = (p + 2 * m) % m
        far = p // (m // 2)
        return ((1 - far) * 2 * p + far * (2 * (m - 1 - p) + 1)) * lanes + lane

    right, left = index_of(pos + 1, core), index_of(pos - 1, core)
    targets = (right, left)[:ways]
    partner = index_of(pos, 1 - core)

    loads = [
        pltpu.make_async_copy(k_hbm, wkv.at[me, :, pl.ds(0, hd)], in_sem.at[0]),
        pltpu.make_async_copy(v_hbm, wkv.at[me, :, pl.ds(hd, hd)], in_sem.at[1]),
        pltpu.make_async_copy(old_hbm, own_ref.at[:, pl.ds(0, (group - 1) * hd)], in_sem.at[2]),
        pltpu.make_async_copy(fresh_hbm, own_ref.at[:, pl.ds((group - 1) * hd, hd)], in_sem.at[3]),
        pltpu.make_async_copy(x_hbm, x_ref, in_sem.at[4]),
        pltpu.make_async_copy(g_hbm, g_ref, in_sem.at[5]),
    ]
    for load in loads:
        load.start()

    barrier = pltpu.get_barrier_semaphore()
    peers = [(right, head), (left, head), (partner, head)]
    peers += [(me, (head + j) % n_head) for j in range(1, n_head)]
    for peer in peers:
        pl.semaphore_signal(barrier, inc=1, device_id=peer, device_id_type=MESH)

    def part_of(p, w, owner):
        return bufs[p].at[owner, pl.ds(w * piece, piece)]

    def ring(p, w, s):
        ref = part_of(p, w, index_of(pos - signs[w] * s, core))
        return pltpu.make_async_remote_copy(
            ref, ref, rs.at[w * 2 + p, s], rr.at[w * 2 + p, s],
            device_id=(targets[w], head), device_id_type=MESH)

    def ring_in(p, w, s):
        ref = part_of(p, w, index_of(pos - signs[w] * (s + 1), core))
        return pltpu.make_async_remote_copy(
            ref, ref, rs.at[w * 2 + p, s], rr.at[w * 2 + p, s],
            device_id=(targets[w], head), device_id_type=MESH)

    def across(p, w, s, lane):
        ref = part_of(p, w, index_of(pos - signs[w] * s, lane))
        return pltpu.make_async_remote_copy(
            ref, ref, cs.at[w * 2 + p, s], cr.at[w * 2 + p, s],
            device_id=(partner, head), device_id_type=MESH)

    def relay(j):
        return pltpu.make_async_remote_copy(
            parcel.at[j - 1], arrived.at[j - 1], hs.at[j - 1], hr.at[j - 1],
            device_id=(me, (head + j) % n_head), device_id_type=MESH)

    shift = [(n_head - src_ref[k] // group) % n_head for k in range(group)]
    taken = [src_ref[k] % group for k in range(group)]
    slot = [
        sum([(shift[l] == shift[k]).astype(jnp.int32) for l in range(k)], jnp.int32(0))
        for k in range(group)
    ]

    def flag(cond):
        return jnp.where(cond, 1.0, 0.0).astype(jnp.float32)

    for load in loads[2:4]:
        load.wait()
    for j in range(1, n_head):
        for c in range(capacity):
            total = jnp.zeros((rows, hd), jnp.float32)
            for c_m in range(group):
                weight = sum(
                    [flag((shift[k] == j) & (slot[k] == c) & (taken[k] == c_m)) for k in range(group)],
                    jnp.float32(0))
                total = total + own_ref[:, c_m * hd:(c_m + 1) * hd].astype(jnp.float32) * weight
            parcel[j - 1, c] = total.astype(jnp.bfloat16)
    for load in loads[:2]:
        load.wait()
    pl.semaphore_wait(barrier, len(peers))
    for j in range(1, n_head):
        relay(j).start()
    for w in range(ways):
        ring(0, w, 0).start()
    for w in range(ways):
        across(0, w, 0, core).start()

    for load in loads[4:]:
        load.wait()
    accq[...] = jnp.zeros_like(accq)
    acckv[...] = jnp.zeros_like(acckv)

    def add(p, w, owner):
        xs = x_ref[:, pl.ds(pl.multiple_of(owner * rows + w * piece, 128), piece)]
        acc = (acckv, accq)[p]
        acc[...] += dot(xs, bufs[p][owner, pl.ds(w * piece, piece), :], 1, 0)

    for j in range(1, n_head):
        relay(j).wait_recv()
    for k in range(group):
        total = jnp.zeros((rows, hd), jnp.float32)
        for c_m in range(group):
            weight = flag((shift[k] == 0) & (taken[k] == c_m))
            total = total + own_ref[:, c_m * hd:(c_m + 1) * hd].astype(jnp.float32) * weight
        for j in range(1, n_head):
            for c in range(capacity):
                weight = flag((shift[k] == j) & (slot[k] == c))
                total = total + arrived[j - 1, c].astype(jnp.float32) * weight
        wq[me, :, k * hd:(k + 1) * hd] = total.astype(jnp.bfloat16)
    for w in range(ways):
        ring(1, w, 0).start()
    for w in range(ways):
        across(1, w, 0, core).start()
    for w in range(ways):
        for p in range(2):
            add(p, w, me)

    def step(s, carry):
        for p in range(2):
            for w in range(ways):
                ring_in(p, w, s - 1).wait_recv()

                @pl.when(s < m - 1)
                def _():
                    ring(p, w, s).start()

                across(p, w, s, core).start()
        for w in range(ways):
            for p in range(2):
                add(p, w, index_of(pos - signs[w] * s, core))
        for w in range(ways):
            for p in range(2):
                across(p, w, s - 1, 1 - core).wait_recv()
        for w in range(ways):
            for p in range(2):
                add(p, w, index_of(pos - signs[w] * (s - 1), 1 - core))
        return carry

    lax.fori_loop(1, m, step, 0)
    for w in range(ways):
        for p in range(2):
            across(p, w, m - 1, 1 - core).wait_recv()
            add(p, w, index_of(pos - signs[w] * (m - 1), 1 - core))

    scale = 1.0 / math.sqrt(hd)
    cosine, sine = cos_ref[...], sin_ref[...]

    def rotate(f):
        return f * cosine + pltpu.roll(f, hd // 2, 1) * sine

    def rotate_back(f):
        return f * cosine - pltpu.roll(f, hd // 2, 1) * sine

    docs = jnp.broadcast_to(doc_ref[...].astype(jnp.float32), (length, length))
    at_key = lax.broadcasted_iota(jnp.int32, (length, length), 1)
    at_query = lax.broadcasted_iota(jnp.int32, (length, length), 0)
    allowed = (at_key <= at_query) & (docs == docs.T)
    key = rotate(acckv[:, :hd]).astype(jnp.bfloat16)
    value = acckv[:, hd:].astype(jnp.bfloat16)
    dkey = jnp.zeros((length, hd), jnp.float32)
    dvalue = jnp.zeros((length, hd), jnp.float32)
    for k in range(group):
        cols = slice(k * hd, (k + 1) * hd)
        query = rotate(accq[:, cols]).astype(jnp.bfloat16)
        given = g_ref[:, cols]
        scores = jnp.where(allowed, dot(query, key, 1, 1) * scale, neg_large)
        weights = jnp.exp(scores - jnp.max(scores, axis=-1, keepdims=True))
        probs = weights / jnp.sum(weights, axis=-1, keepdims=True)
        probs_b = probs.astype(jnp.bfloat16)
        out_ref[:, cols] = dot(probs_b, value, 1, 0).astype(jnp.bfloat16)
        prob_grad = dot(given, value, 1, 1)
        centre = jnp.sum(probs * prob_grad, axis=-1, keepdims=True)
        dscore = (probs * (prob_grad - centre) * scale).astype(jnp.bfloat16)
        dq_ref[:, cols] = rotate_back(dot(dscore, key, 1, 0)).astype(jnp.bfloat16)
        dkey = dkey + dot(dscore, query, 0, 0)
        dvalue = dvalue + dot(probs_b, given, 0, 0)
    dkv_ref[:, :hd] = rotate_back(dkey).astype(jnp.bfloat16)
    dkv_ref[:, hd:] = dvalue.astype(jnp.bfloat16)

    chunks = n_dp // n_head

    def partial(owner):
        return (dot(dq_ref[...], wq[owner], 1, 1) + dot(dkv_ref[...], wkv[owner], 1, 1)).astype(
            jnp.bfloat16)

    def share(j, i):
        return pltpu.make_async_remote_copy(
            psend.at[j - 1, i], precv.at[j - 1, i], ps.at[j - 1, i], pr.at[j - 1, i],
            device_id=(me, (head + j) % n_head), device_id_type=MESH)

    for j in range(1, n_head):
        def send_chunk(i, carry):
            psend[j - 1, i] = partial(((head + j) % n_head) * chunks + i)
            share(j, i).start()
            return carry

        lax.fori_loop(0, chunks, send_chunk, 0)

    def own_chunk(i, carry):
        cols = pl.ds(pl.multiple_of(i * rows, 128), rows)
        grad_ref[:, cols] = partial(head * chunks + i)
        return carry

    lax.fori_loop(0, chunks, own_chunk, 0)

    def finish(i, carry):
        cols = pl.ds(pl.multiple_of(i * rows, 128), rows)
        total = grad_ref[:, cols].astype(jnp.float32)
        for j in range(1, n_head):
            share(j, i).wait_recv()
            total = total + precv[j - 1, i].astype(jnp.float32)
        grad_ref[:, cols] = total.astype(jnp.bfloat16)
        return carry

    lax.fori_loop(0, chunks, finish, 0)

    def drain(s, carry):
        for p in range(2):
            for w in range(ways):
                @pl.when(s < m - 1)
                def _():
                    ring(p, w, s).wait_send()

                across(p, w, s, core).wait_send()
        return carry

    lax.fori_loop(0, m, drain, 0)
    for j in range(1, n_head):
        relay(j).wait_send()

        def drain_share(i, carry):
            share(j, i).wait_send()
            return carry

        lax.fori_loop(0, chunks, drain_share, 0)


def solution(mesh):
    n_dp, n_head = mesh.shape["dp"], mesh.shape["head"]

    def local(x, old, fresh, wk, wv, g, head_source, doc_ids):
        length, width = x.shape
        rows, hd = wk.shape
        group = g.shape[1] // hd
        ways = 2 if rows % 256 == 0 else 1
        m = n_dp // 2
        capacity = (group + n_head - 1) // n_head
        chunks = n_dp // n_head
        cosine, sine = rotary_tables(length, hd)
        bf, f32 = jnp.bfloat16, jnp.float32
        vm = pl.BlockSpec(memory_space=pltpu.VMEM)
        anyspace = pl.BlockSpec(memory_space=pl.ANY)
        dma = pltpu.SemaphoreType.DMA
        return pl.pallas_call(
            functools.partial(kernel, n_dp, n_head, group, ways),
            out_shape=(
                jax.ShapeDtypeStruct((length, group * hd), bf),
                jax.ShapeDtypeStruct((length, width // n_head), bf),
            ),
            in_specs=[pl.BlockSpec(memory_space=pltpu.SMEM), vm, vm, vm] + [anyspace] * 6,
            out_specs=(vm, vm),
            scratch_shapes=[
                pltpu.VMEM((length, width), bf),
                pltpu.VMEM((rows, group * hd), bf),
                pltpu.VMEM((length, group * hd), bf),
                pltpu.VMEM((n_dp, rows, group * hd), bf),
                pltpu.VMEM((n_dp, rows, 2 * hd), bf),
                pltpu.VMEM((n_head - 1, capacity, rows, hd), bf),
                pltpu.VMEM((n_head - 1, capacity, rows, hd), bf),
                pltpu.VMEM((length, group * hd), f32),
                pltpu.VMEM((length, 2 * hd), f32),
                pltpu.VMEM((length, group * hd), bf),
                pltpu.VMEM((length, 2 * hd), bf),
                pltpu.VMEM((n_head - 1, chunks, length, rows), bf),
                pltpu.VMEM((n_head - 1, chunks, length, rows), bf),
                dma((6,)),
                dma((2 * ways, m)),
                dma((2 * ways, m)),
                dma((2 * ways, m)),
                dma((2 * ways, m)),
                dma((n_head - 1,)),
                dma((n_head - 1,)),
                dma((n_head - 1, chunks)),
                dma((n_head - 1, chunks)),
            ],
            compiler_params=pltpu.CompilerParams(
                collective_id=0, has_side_effects=True, vmem_limit_bytes=50 * 1024 * 1024),
        )(head_source, doc_ids.reshape(1, -1), cosine, sine, x, old, fresh, wk, wv, g)

    in_specs = (
        P("dp", None), P("dp", "head"), P("dp", "head"), P("dp", "head"),
        P("dp", "head"), P("dp", "head"), P(), P("dp"),
    )
    return jax.shard_map(
        local, mesh=mesh, in_specs=in_specs,
        out_specs=(P("dp", "head"), P("dp", "head")), check_vma=False)
```

time: 253 us -> 124 us (0.49)
  waiting for transfers between devices: 189 us -> 0 us
  Pallas kernels: 0 us -> 114 us
  matrix products: 32.1 us -> 0 us
  between operations: 14 us -> 0.66 us
  starting transfers between devices: 4.65 us -> 0 us
  other arithmetic: 4.3 us -> 0 us
    all_gather x3 -> x0, waiting for transfers between devices: 147 us -> none  [the longest x1 88.9 us: local(): lax.all_gather(local_heads.reshape(shard_rows, group_size * head_dim), 'd...]
    pallas_call x0 -> x1, Pallas kernels: none -> 114 us  [local(): pl.pallas_call(functools.partial(kernel, n_dp, n_head, group, ways), out_...]
    dot_general x12 -> x0, matrix products: 30.8 us -> none  [the longest x1 5.98 us: local(): jnp.einsum('sc,wc->sw', dquery.reshape(length, group_size * head_dim), wq...]
    reduce_scatter x1 -> x0, waiting for transfers between devices: 28 us -> none  [local(): lax.psum_scatter(partial_grad.astype(jnp.bfloat16), 'head', scatter_dimen...]
    all_to_all x1 -> x0, waiting for transfers between devices: 12.3 us -> none  [local(): lax.all_to_all(parcel, 'head', split_axis=0, concat_axis=0, tiled=True)]
    unnamed x28 -> x20, local copies, waits for them, and re-layouts: 3.24 us -> 9.29 us
    all_to_all x1 -> x0, starting transfers between devices: 4.31 us -> none  [local(): lax.all_to_all(parcel, 'head', split_axis=0, concat_axis=0, tiled=True)]
    another operation x4 -> x0, other arithmetic: 2.75 us -> none
  transfers between devices with their start and end apart: 5 -> 0, of which waited for: 5 -> 0; matrix products, arithmetic and copies ran while one was open for 7% -> 0% of each run, Pallas kernels for 0% -> 0%
where the time goes in v1:
time: 124 us
  Pallas kernels  114 us (92%)
  local copies, waits for them, and re-layouts  9.29 us (7%)
    pallas_call x1, Pallas kernels, local(): pl.pallas_call(functools.partial(kernel, n_dp, n_head, group, ways), out_...  114 us
    unnamed x20, local copies, waits for them, and re-layouts  9.29 us

profile of v1, /device:TPU:0, one launch (start us, length us, event | category | flops | bytes accessed | tf_op | source)
XLA Modules:
  0.0 123.9 jit_solution(14963621883031666667)
XLA Ops:
  0.6 0.0 copy-start
  0.6 1.0 copy-done
  1.7 0.0 copy-start.1
  1.7 0.9 copy-done.1
  2.6 0.0 copy-start.2
  2.6 0.9 copy-done.2
  3.5 0.0 copy-start.3
  3.5 0.9 copy-done.3
  4.4 0.0 copy-start.4
  4.4 0.9 copy-done.4
  5.3 0.0 copy-start.5
  5.3 0.8 copy-done.5
  6.1 0.0 copy-start.6
  6.1 0.8 copy-done.6
  7.0 0.0 copy-start.7
  7.0 0.7 copy-done.7
  7.6 0.0 copy-start.8
  7.6 0.7 copy-done.8
  8.3 113.9 %shard_map.113 = (bf16[128,640]{1,0:T(8,128)(2,1)S(1)}, bf16[128,4096]{1,0:T(8,128)(2,1)S(1)}) custom-call(s32[10]{0:T(128)S(1)} %copy-done.7, s32[1,128]{1,0:T(1,128)S(1)} %bitcast.1, f32[128,128]{1,0:T(8,128)S(1)} %copy-done.6, f32[128,128]{1,0:T(8,128)S(1)} %copy-done.5, bf16[128,8192]{1,0:T(8,128)(2,1)} %x_hbm.1, bf16[512,512]{1,0:T(8,128)(2,1)S(1)} %copy-done, ...), custom_call_target="tpu_custom_call" | custom-call | tf_op jit(solution)/shard_map/pallas_call | solution.py:304
  122.3 0.7 copy.14
  122.9 1.0 copy.15
Async XLA Ops:
  0.6 1.0 copy-start
  1.7 0.9 copy-start.1
  2.6 0.9 copy-start.2
  3.5 0.9 copy-start.3
  4.4 0.9 copy-start.4
  5.3 0.8 copy-start.5
  6.1 0.8 copy-start.6
  7.0 0.7 copy-start.7
  7.6 0.7 copy-start.8

commit v2 on v1

--- a/solution.py
+++ b/solution.py
@@ -48,9 +48,13 @@
     side, level = chip % 2, chip // 2
     pos = (1 - side) * level + side * (m - 1 - level)
     piece = rows // ways
-    capacity = parcel.shape[1]
+    sub = piece // 2
+    lead = min(2, m - 2)
+    parts = 3
+    capacity = parcel.shape[2]
     signs = (1, -1)[:ways]
     bufs = (wkv, wq)
+    spans = ((0, piece), (0, sub), (sub, sub))
 
     def index_of(p, lane):
         p = (p + 2 * m) % m
@@ -79,29 +83,30 @@
         pl.semaphore_signal(barrier, inc=1, device_id=peer, device_id_type=MESH)
 
     def part_of(p, w, owner):
-        return bufs[p].at[owner, pl.ds(w * piece, piece)]
+        first, count = spans[p]
+        return bufs[min(p, 1)].at[owner, pl.ds(w * piece + first, count)]
 
     def ring(p, w, s):
         ref = part_of(p, w, index_of(pos - signs[w] * s, core))
         return pltpu.make_async_remote_copy(
-            ref, ref, rs.at[w * 2 + p, s], rr.at[w * 2 + p, s],
+            ref, ref, rs.at[w * parts + p, s], rr.at[w * parts + p, s],
             device_id=(targets[w], head), device_id_type=MESH)
 
     def ring_in(p, w, s):
         ref = part_of(p, w, index_of(pos - signs[w] * (s + 1), core))
         return pltpu.make_async_remote_copy(
-            ref, ref, rs.at[w * 2 + p, s], rr.at[w * 2 + p, s],
+            ref, ref, rs.at[w * parts + p, s], rr.at[w * parts + p, s],
             device_id=(targets[w], head), device_id_type=MESH)
 
     def across(p, w, s, lane):
         ref = part_of(p, w, index_of(pos - signs[w] * s, lane))
         return pltpu.make_async_remote_copy(
-            ref, ref, cs.at[w * 2 + p, s], cr.at[w * 2 + p, s],
+            ref, ref, cs.at[w * parts + p, s], cr.at[w * parts + p, s],
             device_id=(partner, head), device_id_type=MESH)
 
-    def relay(j):
-        return pltpu.make_async_remote_copy(
-            parcel.at[j - 1], arrived.at[j - 1], hs.at[j - 1], hr.at[j - 1],
+    def relay(u, j):
+        return pltpu.make_async_remote_copy(
+            parcel.at[u, j - 1], arrived.at[u, j - 1], hs.at[u, j - 1], hr.at[u, j - 1],
             device_id=(me, (head + j) % n_head), device_id_type=MESH)
 
     shift = [(n_head - src_ref[k] // group) % n_head for k in range(group)]
@@ -114,27 +119,38 @@
     def flag(cond):
         return jnp.where(cond, 1.0, 0.0).astype(jnp.float32)
 
-    for load in loads[2:4]:
-        load.wait()
-    for j in range(1, n_head):
-        for c in range(capacity):
-            total = jnp.zeros((rows, hd), jnp.float32)
-            for c_m in range(group):
-                weight = sum(
-                    [flag((shift[k] == j) & (slot[k] == c) & (taken[k] == c_m)) for k in range(group)],
-                    jnp.float32(0))
-                total = total + own_ref[:, c_m * hd:(c_m + 1) * hd].astype(jnp.float32) * weight
-            parcel[j - 1, c] = total.astype(jnp.bfloat16)
+    units = [w * 2 + half for half in range(2) for w in range(ways)]
+
+    def weigh(u, weights):
+        total = jnp.zeros((sub, hd), jnp.float32)
+        for c_m in range(group):
+            block = own_ref[u * sub:(u + 1) * sub, c_m * hd:(c_m + 1) * hd]
+            total = total + block.astype(jnp.float32) * weights[c_m]
+        return total.astype(jnp.bfloat16)
+
     for load in loads[:2]:
         load.wait()
     pl.semaphore_wait(barrier, len(peers))
-    for j in range(1, n_head):
-        relay(j).start()
     for w in range(ways):
         ring(0, w, 0).start()
     for w in range(ways):
         across(0, w, 0, core).start()
-
+    for load in loads[2:4]:
+        load.wait()
+    for u in units:
+        for j in range(1, n_head):
+            for c in range(capacity):
+                weights = [
+                    sum([flag((shift[k] == j) & (slot[k] == c) & (taken[k] == c_m))
+                         for k in range(group)], jnp.float32(0))
+                    for c_m in range(group)
+                ]
+                parcel[u, j - 1, c] = weigh(u, weights)
+            relay(u, j).start()
+    for k in range(group):
+        weights = [flag((shift[k] == 0) & (taken[k] == c_m)) for c_m in range(group)]
+        for u in units:
+            wq[me, u * sub:(u + 1) * sub, k * hd:(k + 1) * hd] = weigh(u, weights)
     for load in loads[4:]:
         load.wait()
     accq[...] = jnp.zeros_like(accq)
@@ -145,41 +161,57 @@
         acc = (acckv, accq)[p]
         acc[...] += dot(xs, bufs[p][owner, pl.ds(w * piece, piece), :], 1, 0)
 
-    for j in range(1, n_head):
-        relay(j).wait_recv()
-    for k in range(group):
-        total = jnp.zeros((rows, hd), jnp.float32)
-        for c_m in range(group):
-            weight = flag((shift[k] == 0) & (taken[k] == c_m))
-            total = total + own_ref[:, c_m * hd:(c_m + 1) * hd].astype(jnp.float32) * weight
+    def pass_on(p, w, s):
+        ring_in(p, w, s - 1).wait_recv()
+
+        @pl.when(s < m - 1)
+        def _():
+            ring(p, w, s).start()
+
+        across(p, w, s, core).start()
+
+    def unit_out(u):
+        block = pl.ds(u * sub, sub)
         for j in range(1, n_head):
-            for c in range(capacity):
-                weight = flag((shift[k] == j) & (slot[k] == c))
-                total = total + arrived[j - 1, c].astype(jnp.float32) * weight
-        wq[me, :, k * hd:(k + 1) * hd] = total.astype(jnp.bfloat16)
-    for w in range(ways):
-        ring(1, w, 0).start()
-    for w in range(ways):
-        across(1, w, 0, core).start()
-    for w in range(ways):
-        for p in range(2):
-            add(p, w, me)
+            relay(u, j).wait_recv()
+        for k in range(group):
+            cols = slice(k * hd, (k + 1) * hd)
+            total = wq[me, block, cols].astype(jnp.float32)
+            for j in range(1, n_head):
+                for c in range(capacity):
+                    weight = flag((shift[k] == j) & (slot[k] == c))
+                    total = total + arrived[u, j - 1, c].astype(jnp.float32) * weight
+            wq[me, block, cols] = total.astype(jnp.bfloat16)
+        ring(1 + u % 2, u // 2, 0).start()
+        across(1 + u % 2, u // 2, 0, core).start()
+
+    for w in range(ways):
+        add(0, w, me)
+    for u in units[:ways]:
+        unit_out(u)
+    for s in range(1, lead + 1):
+        for w in range(ways):
+            pass_on(0, w, s)
+        if s == 1:
+            for u in units[ways:]:
+                unit_out(u)
+    for w in range(ways):
+        add(1, w, me)
 
     def step(s, carry):
-        for p in range(2):
+        @pl.when(s + lead < m)
+        def _():
             for w in range(ways):
-                ring_in(p, w, s - 1).wait_recv()
-
-                @pl.when(s < m - 1)
-                def _():
-                    ring(p, w, s).start()
-
-                across(p, w, s, core).start()
+                pass_on(0, w, s + lead)
+
+        for p in range(1, parts):
+            for w in range(ways):
+                pass_on(p, w, s)
         for w in range(ways):
             for p in range(2):
                 add(p, w, index_of(pos - signs[w] * s, core))
         for w in range(ways):
-            for p in range(2):
+            for p in range(parts):
                 across(p, w, s - 1, 1 - core).wait_recv()
         for w in range(ways):
             for p in range(2):
@@ -188,8 +220,9 @@
 
     lax.fori_loop(1, m, step, 0)
     for w in range(ways):
+        for p in range(parts):
+            across(p, w, m - 1, 1 - core).wait_recv()
         for p in range(2):
-            across(p, w, m - 1, 1 - core).wait_recv()
             add(p, w, index_of(pos - signs[w] * (m - 1), 1 - core))
 
     scale = 1.0 / math.sqrt(hd)
@@ -265,7 +298,7 @@
     lax.fori_loop(0, chunks, finish, 0)
 
     def drain(s, carry):
-        for p in range(2):
+        for p in range(parts):
             for w in range(ways):
                 @pl.when(s < m - 1)
                 def _():
@@ -276,7 +309,8 @@
 
     lax.fori_loop(0, m, drain, 0)
     for j in range(1, n_head):
-        relay(j).wait_send()
+        for u in units:
+            relay(u, j).wait_send()
 
         def drain_share(i, carry):
             share(j, i).wait_send()
@@ -315,8 +349,8 @@
                 pltpu.VMEM((length, group * hd), bf),
                 pltpu.VMEM((n_dp, rows, group * hd), bf),
                 pltpu.VMEM((n_dp, rows, 2 * hd), bf),
-                pltpu.VMEM((n_head - 1, capacity, rows, hd), bf),
-                pltpu.VMEM((n_head - 1, capacity, rows, hd), bf),
+                pltpu.VMEM((2 * ways, n_head - 1, capacity, rows // (2 * ways), hd), bf),
+                pltpu.VMEM((2 * ways, n_head - 1, capacity, rows // (2 * ways), hd), bf),
                 pltpu.VMEM((length, group * hd), f32),
                 pltpu.VMEM((length, 2 * hd), f32),
                 pltpu.VMEM((length, group * hd), bf),
@@ -324,12 +358,12 @@
                 pltpu.VMEM((n_head - 1, chunks, length, rows), bf),
                 pltpu.VMEM((n_head - 1, chunks, length, rows), bf),
                 dma((6,)),
-                dma((2 * ways, m)),
-                dma((2 * ways, m)),
-                dma((2 * ways, m)),
-                dma((2 * ways, m)),
-                dma((n_head - 1,)),
-                dma((n_head - 1,)),
+                dma((3 * ways, m)),
+                dma((3 * ways, m)),
+                dma((3 * ways, m)),
+                dma((3 * ways, m)),
+                dma((2 * ways, n_head - 1)),
+                dma((2 * ways, n_head - 1)),
                 dma((n_head - 1, chunks)),
                 dma((n_head - 1, chunks)),
             ],

time: 124 us -> 120 us (0.968)
  Pallas kernels: 114 us -> 110 us
    pallas_call x1, Pallas kernels: 114 us -> 110 us  [local(): pl.pallas_call(functools.partial(kernel, n_dp, n_head, group, ways), out_...]
where the time goes in v2:
time: 120 us
  Pallas kernels  110 us (92%)
  local copies, waits for them, and re-layouts  9.29 us (8%)
    pallas_call x1, Pallas kernels, local(): pl.pallas_call(functools.partial(kernel, n_dp, n_head, group, ways), out_...  110 us
    unnamed x20, local copies, waits for them, and re-layouts  9.29 us

profile of v2, /device:TPU:0, one launch (start us, length us, event | category | flops | bytes accessed | tf_op | source)
XLA Modules:
  0.0 120.0 jit_solution(238732088460863663)
XLA Ops:
  0.6 0.0 copy-start
  0.6 1.0 copy-done
  1.7 0.0 copy-start.1
  1.7 0.9 copy-done.1
  2.6 0.0 copy-start.2
  2.6 0.9 copy-done.2
  3.5 0.0 copy-start.3
  3.5 0.9 copy-done.3
  4.4 0.0 copy-start.4
  4.4 0.9 copy-done.4
  5.3 0.0 copy-start.5
  5.3 0.8 copy-done.5
  6.1 0.0 copy-start.6
  6.1 0.8 copy-done.6
  7.0 0.0 copy-start.7
  7.0 0.7 copy-done.7
  7.6 0.0 copy-start.8
  7.6 0.7 copy-done.8
  8.3 110.1 %shard_map.113 = (bf16[128,640]{1,0:T(8,128)(2,1)S(1)}, bf16[128,4096]{1,0:T(8,128)(2,1)S(1)}) custom-call(s32[10]{0:T(128)S(1)} %copy-done.7, s32[1,128]{1,0:T(1,128)S(1)} %bitcast.1, f32[128,128]{1,0:T(8,128)S(1)} %copy-done.6, f32[128,128]{1,0:T(8,128)S(1)} %copy-done.5, bf16[128,8192]{1,0:T(8,128)(2,1)} %x_hbm.1, bf16[512,512]{1,0:T(8,128)(2,1)S(1)} %copy-done, ...), custom_call_target="tpu_custom_call" | custom-call | tf_op jit(solution)/shard_map/pallas_call | solution.py:338
  118.4 0.7 copy.14
  119.1 1.0 copy.15
Async XLA Ops:
  0.6 1.0 copy-start
  1.7 0.9 copy-start.1
  2.6 0.9 copy-start.2
  3.5 0.9 copy-start.3
  4.4 0.9 copy-start.4
  5.3 0.8 copy-start.5
  6.1 0.8 copy-start.6
  7.0 0.7 copy-start.7
  7.6 0.7 copy-start.8

commit v3 on v2

--- a/solution.py
+++ b/solution.py
@@ -33,9 +33,9 @@
 
 def kernel(
     n_dp, n_head, group, ways,
-    src_ref, doc_ref, cos_ref, sin_ref, x_hbm, old_hbm, fresh_hbm, k_hbm, v_hbm, g_hbm,
+    src_ref, doc_hbm, cos_hbm, sin_hbm, x_hbm, old_hbm, fresh_hbm, k_hbm, v_hbm, g_hbm,
     out_ref, grad_ref,
-    x_ref, own_ref, g_ref, wq, wkv, parcel, arrived, accq, acckv, dq_ref, dkv_ref,
+    doc_ref, cos_ref, sin_ref, x_ref, own_ref, g_ref, wq, wkv, parcel, arrived, accq, acckv, dq_ref, dkv_ref,
     psend, precv,
     in_sem, rs, rr, cs, cr, hs, hr, ps, pr,
 ):
@@ -72,6 +72,9 @@
         pltpu.make_async_copy(fresh_hbm, own_ref.at[:, pl.ds((group - 1) * hd, hd)], in_sem.at[3]),
         pltpu.make_async_copy(x_hbm, x_ref, in_sem.at[4]),
         pltpu.make_async_copy(g_hbm, g_ref, in_sem.at[5]),
+        pltpu.make_async_copy(doc_hbm, doc_ref, in_sem.at[6]),
+        pltpu.make_async_copy(cos_hbm, cos_ref, in_sem.at[7]),
+        pltpu.make_async_copy(sin_hbm, sin_ref, in_sem.at[8]),
     ]
     for load in loads:
         load.start()
@@ -341,9 +344,12 @@
                 jax.ShapeDtypeStruct((length, group * hd), bf),
                 jax.ShapeDtypeStruct((length, width // n_head), bf),
             ),
-            in_specs=[pl.BlockSpec(memory_space=pltpu.SMEM), vm, vm, vm] + [anyspace] * 6,
+            in_specs=[pl.BlockSpec(memory_space=pltpu.SMEM)] + [anyspace] * 9,
             out_specs=(vm, vm),
             scratch_shapes=[
+                pltpu.VMEM((1, length), jnp.int32),
+                pltpu.VMEM((length, hd), f32),
+                pltpu.VMEM((length, hd), f32),
                 pltpu.VMEM((length, width), bf),
                 pltpu.VMEM((rows, group * hd), bf),
                 pltpu.VMEM((length, group * hd), bf),
@@ -357,7 +363,7 @@
                 pltpu.VMEM((length, 2 * hd), bf),
                 pltpu.VMEM((n_head - 1, chunks, length, rows), bf),
                 pltpu.VMEM((n_head - 1, chunks, length, rows), bf),
-                dma((6,)),
+                dma((9,)),
                 dma((3 * ways, m)),
                 dma((3 * ways, m)),
                 dma((3 * ways, m)),
@@ -368,7 +374,7 @@
                 dma((n_head - 1, chunks)),
             ],
             compiler_params=pltpu.CompilerParams(
-                collective_id=0, has_side_effects=True, vmem_limit_bytes=50 * 1024 * 1024),
+                collective_id=0, has_side_effects=True, vmem_limit_bytes=67043328),
         )(head_source, doc_ids.reshape(1, -1), cosine, sine, x, old, fresh, wk, wv, g)
 
     in_specs = (

time: 120 us -> 116 us (0.967)
  local copies, waits for them, and re-layouts: 9.29 us -> 3.88 us
    unnamed x20 -> x2, local copies, waits for them, and re-layouts: 9.29 us -> 3.88 us
where the time goes in v3:
time: 116 us
  Pallas kernels  111 us (96%)
  local copies, waits for them, and re-layouts  3.88 us (3%)
    pallas_call x1, Pallas kernels, local(): pl.pallas_call(functools.partial(kernel, n_dp, n_head, group, ways), out_...  111 us
    unnamed x2, local copies, waits for them, and re-layouts  3.88 us

profile of v3, /device:TPU:0, one launch (start us, length us, event | category | flops | bytes accessed | tf_op | source)
XLA Modules:
  0.0 115.6 jit_solution(1368733778250696503)
XLA Ops:
  0.6 111.1 %shard_map.113 = (bf16[128,640]{1,0:T(8,128)(2,1)}, bf16[128,4096]{1,0:T(8,128)(2,1)}) custom-call(s32[10]{0:T(128)} %src_ref.1, s32[1,128]{1,0:T(1,128)} %bitcast.1, f32[128,128]{1,0:T(8,128)} %constant.4.clone.cos_hbm, f32[128,128]{1,0:T(8,128)} %constant.5.clone.sin_hbm, bf16[128,8192]{1,0:T(8,128)(2,1)} %x_hbm.1, bf16[512,512]{1,0:T(8,128)(2,1)} %old_hbm.1, ...), custom_call_target="tpu_custom_call" | custom-call | tf_op jit(solution)/shard_map/pallas_call | solution.py:341
  111.7 1.6 %copy.14 = bf16[128,640]{1,0:T(8,128)(2,1)} copy(bf16[128,640]{1,0:T(8,128)(2,1)} %get-tuple-element.4) | data formatting | bytes 327680
  113.3 2.3 %copy.15 = bf16[128,4096]{1,0:T(8,128)(2,1)} copy(bf16[128,4096]{1,0:T(8,128)(2,1)} %get-tuple-element.5) | data formatting | bytes 2097152
